TPU v7x, 32 devices: a whole 2x2x4 slice. The times are simulated.
32 devices in a mesh: vid: 2 (over x), tm: 16 (over z, y, core).
Axes of the slice: x: 2, y: 2, z: 4, core: 2. Of those that a mesh axis runs over, the one named last changes fastest.
Arguments:
- queries: bfloat16 [4096, 1536], P(('vid', 'tm')), parts along dimension 0, may hold values from -6 to 6
- keys: bfloat16 [4096, 1536], P(('vid', 'tm')), parts along dimension 0, may hold values from -6 to 6
- values: bfloat16 [4096, 1536], P(('vid', 'tm')), parts along dimension 0, may hold values from -6 to 6
- far_picks: int32 [64, 8], P(('vid', 'tm')), parts along dimension 0, may hold values from 0 to 1
- out_weight: bfloat16 [1536, 1536], replicated, may hold values from -0.15625 to 0.15625
Outputs:
- mixed: bfloat16 [4096, 1536], P(('vid', 'tm')), parts along dimension 0
There are 2 independent parts, one for each index of `vid`. A program takes and returns all parts, laid end to end along the dimension named above; an argument that names none is the same for every part. Nothing has to cross between parts.
All inputs are finite; a program needn't handle non-finite values.
Results may differ from a plain program's by a relative error of at most 0.0056.
Values may be sent and summed in bfloat16 or wider, within the bound.
A program may use at most 64 MiB of HBM per device.

v0:
```python
import jax
import jax.numpy as jnp
from jax import lax
from jax.sharding import PartitionSpec as P

HEADS = 12
HEAD_DIM = 128
BLK = 64
LEVELS = 2
PICKS = 2
FAR = 8


def padded(cells, sides, width):
    for axis, dim in sides:
        count = lax.axis_size(axis)
        ends = count - 1
        head = lax.slice_in_dim(cells, 0, width, axis=dim)
        tail = lax.slice_in_dim(cells, cells.shape[dim] - width, cells.shape[dim], axis=dim)
        cells = jnp.concatenate(
            [
                lax.ppermute(tail, axis, [(i, (i + 1) % count) for i in range(ends)]),
                cells,
                lax.ppermute(head, axis, [((i + 1) % count, i) for i in range(ends)]),
            ],
            axis=dim,
        )
    return cells


def shifted(block, axis, distance):
    devices = range(lax.axis_size(axis))
    route = [(i - distance, i) for i in devices if i - distance in devices]
    return lax.ppermute(block, axis, route)


def far_offsets():
    offset_list = []
    for column in range(FAR):
        magnitude = 2 ** (1 + column // PICKS % LEVELS)
        offset_list.append(-magnitude if column < FAR // 2 else magnitude)
    return offset_list


def attend(query_rows, near_pair, near_valid, far_pair, far_valid, out_weight):
    blocks = query_rows.shape[0] // BLK
    width = query_rows.shape[1]
    scale = HEAD_DIM ** (-0.5)
    query_heads = query_rows.reshape(blocks, BLK, HEADS, HEAD_DIM)
    near_keys = near_pair[0].reshape(-1, HEADS, HEAD_DIM)
    near_values = near_pair[1].reshape(-1, HEADS, HEAD_DIM)
    far_keys = far_pair[0].reshape(blocks, -1, HEADS, HEAD_DIM)
    far_values = far_pair[1].reshape(blocks, -1, HEADS, HEAD_DIM)
    near_scores = (
        jnp.einsum("bqhd,khd->bhqk", query_heads, near_keys, preferred_element_type=jnp.float32)
        * scale
    )
    near_scores = jnp.where(near_valid, near_scores, jnp.float32(-1e30))
    far_scores = (
        jnp.einsum("bqhd,bkhd->bhqk", query_heads, far_keys, preferred_element_type=jnp.float32)
        * scale
    )
    far_scores = jnp.where(far_valid, far_scores, jnp.float32(-1e30))
    top_score = jnp.maximum(jnp.max(near_scores, -1), jnp.max(far_scores, -1))[..., None]
    near_exp = jnp.exp(near_scores - top_score)
    far_exp = jnp.exp(far_scores - top_score)
    total = jnp.sum(near_exp, -1) + jnp.sum(far_exp, -1)
    summed = jnp.einsum(
        "bhqk,khd->bqhd",
        near_exp.astype(jnp.bfloat16),
        near_values,
        preferred_element_type=jnp.float32,
    )
    summed = summed + jnp.einsum(
        "bhqk,bkhd->bqhd",
        far_exp.astype(jnp.bfloat16),
        far_values,
        preferred_element_type=jnp.float32,
    )
    attended = (
        (summed / jnp.transpose(total, (0, 2, 1))[..., None])
        .reshape(blocks * BLK, width)
        .astype(jnp.bfloat16)
    )
    return jnp.dot(attended, out_weight, preferred_element_type=jnp.float32).astype(jnp.bfloat16)


def body(queries, keys, values, far_picks, out_weight):
    tok_rows = queries.shape[0]
    width = queries.shape[1]
    blocks = tok_rows // BLK
    devices = lax.axis_size("tm")
    device_index = lax.axis_index("tm")
    pair = jnp.stack([keys, values])
    near_pair = padded(pair, (("tm", 1),), tok_rows)
    shards = {}
    for section_level in range(LEVELS):
        distance = 2 ** (section_level + 1)
        for direction in (-1, 1):
            shards[direction * distance] = shifted(pair, "tm", -direction * distance)
    offset_list = far_offsets()
    chosen_list = []
    valid_list = []
    for column in range(FAR):
        offset = offset_list[column]
        source = shards[offset].reshape(2, blocks, BLK, width)
        chosen_list.append(jnp.take(source, far_picks[:, column], axis=1))
        valid_list.append((device_index + offset >= 0) & (device_index + offset < devices))
    far_pair = jnp.stack(chosen_list, 2).reshape(2, blocks, FAR * BLK, width)
    far_valid = jnp.repeat(jnp.stack(valid_list), BLK)
    near_valid = jnp.repeat(
        jnp.stack([device_index > 0, jnp.array(True), device_index < devices - 1]), tok_rows
    )
    return attend(queries, near_pair, near_valid, far_pair, far_valid, out_weight)


def solution(mesh):
    placed = (
        P(("vid", "tm"), None),
        P(("vid", "tm"), None),
        P(("vid", "tm"), None),
        P(("vid", "tm"), None),
        P(),
    )
    return jax.shard_map(
        body, mesh=mesh, in_specs=placed, out_specs=P(("vid", "tm"), None), check_vma=False
    )
```

profile of v0, /device:TPU:15, one launch (start us, length us, event | category | flops | bytes accessed | tf_op | source)
XLA Modules:
  0.0 95.5 jit_solution(6004676493157633338)
XLA Ops:
  0.0 1.3 %copy.56 = bf16[128,1536]{0,1:T(8,128)(2,1)S(1)} copy(bf16[128,1536]{1,0:T(8,128)(2,1)} %param.8) | data formatting | bytes 786432 | tf_op args[1]
  1.3 1.2 %copy.57 = bf16[128,1536]{0,1:T(8,128)(2,1)S(1)} copy(bf16[128,1536]{1,0:T(8,128)(2,1)} %param.9) | data formatting | bytes 786432 | tf_op args[2]
  2.5 1.0 %pad_maximum_fusion.1 = bf16[2,128,1536]{1,2,0:T(8,128)(2,1)} fusion(bf16[1,128,1536]{1,2,0:T(8,128)(2,1)S(1)} %bitcast.116, bf16[1,128,1536]{1,2,0:T(8,128)(2,1)S(1)} %bitcast.114), kind=kLoop, calls=%fused_computation.36 | loop fusion | flops 393216 | bytes 1572864 | tf_op jit(solution)/shard_map/stack | solution.py:94
  3.5 3.1 %collective-permute-start.2 = (bf16[2,128,1536]{1,2,0:T(8,128)(2,1)}, bf16[2,128,1536]{1,2,0:T(8,128)(2,1)S(1)}, u32[]{:S(2)}, u32[]{:S(2)}) collective-permute-start(bf16[2,128,1536]{1,2,0:T(8,128)(2,1)} %pad_maximum_fusion.1), channel_id=1, source_target_pairs={{0,2},{1,3},{2,4},{3,5},{4,6},{5,7},{6,8},{7,9},{8,10},{9,11},{10,... | collective-permute-start | bytes 2359304 | tf_op jit(solution)/shard_map/ppermute | solution.py:34
  6.7 3.2 %collective-permute-start.3 = (bf16[2,128,1536]{1,2,0:T(8,128)(2,1)}, bf16[2,128,1536]{1,2,0:T(8,128)(2,1)S(1)}, u32[]{:S(2)}, u32[]{:S(2)}) collective-permute-start(bf16[2,128,1536]{1,2,0:T(8,128)(2,1)} %pad_maximum_fusion.1), channel_id=1, source_target_pairs={{0,4},{1,5},{2,6},{3,7},{4,8},{5,9},{6,10},{7,11},{8,12},{9,13},{1... | collective-permute-start | bytes 2359304 | tf_op jit(solution)/shard_map/ppermute | solution.py:34
  9.9 2.1 %collective-permute-start.4 = (bf16[2,128,1536]{1,2,0:T(8,128)(2,1)}, bf16[2,128,1536]{1,2,0:T(8,128)(2,1)}, u32[]{:S(2)}, u32[]{:S(2)}) collective-permute-start(bf16[2,128,1536]{1,2,0:T(8,128)(2,1)} %pad_maximum_fusion.1), channel_id=1, source_target_pairs={{2,0},{3,1},{4,2},{5,3},{6,4},{7,5},{8,6},{9,7},{10,8},{11,9},{12,... | collective-permute-start | bytes 2359304 | tf_op jit(solution)/shard_map/ppermute | solution.py:34
  12.0 2.1 %collective-permute-start.5 = (bf16[2,128,1536]{1,2,0:T(8,128)(2,1)}, bf16[2,128,1536]{1,2,0:T(8,128)(2,1)}, u32[]{:S(2)}, u32[]{:S(2)}) collective-permute-start(bf16[2,128,1536]{1,2,0:T(8,128)(2,1)} %pad_maximum_fusion.1), channel_id=1, source_target_pairs={{4,0},{5,1},{6,2},{7,3},{8,4},{9,5},{10,6},{11,7},{12,8},{13,9},{1... | collective-permute-start | bytes 2359304 | tf_op jit(solution)/shard_map/ppermute | solution.py:34
  14.1 5.7 %collective-permute-start = (bf16[2,128,1536]{1,2,0:T(8,128)(2,1)}, bf16[2,128,1536]{1,2,0:T(8,128)(2,1)}, u32[]{:S(2)}, u32[]{:S(2)}) collective-permute-start(bf16[2,128,1536]{1,2,0:T(8,128)(2,1)} %pad_maximum_fusion.1), channel_id=1, source_target_pairs={{0,1},{1,2},{2,3},{3,4},{4,5},{5,6},{6,7},{7,8},{8,9},{9,10},{10,1... | collective-permute-start | bytes 2359304 | tf_op jit(solution)/shard_map/ppermute | solution.py:22
  20.2 0.6 compare_and_fusion.7
  20.7 0.6 pad_clamp_fusion.7
  21.3 0.6 pad_clamp_fusion.6
  22.0 0.6 compare_and_fusion
  22.7 0.6 broadcast_bitcast_fusion
  23.3 0.6 pad_clamp_fusion.1
  24.0 0.6 reshape.45
  25.0 0.9 copy.59
  25.9 0.6 pad_clamp_fusion
  26.5 0.5 compare_and_fusion.5
  27.0 0.6 compare_and_fusion.3
  27.6 0.5 compare_and_fusion.1
  28.1 12.8 %collective-permute-done.2 = bf16[2,128,1536]{1,2,0:T(8,128)(2,1)S(1)} collective-permute-done((bf16[2,128,1536]{1,2,0:T(8,128)(2,1)}, bf16[2,128,1536]{1,2,0:T(8,128)(2,1)S(1)}, u32[]{:S(2)}, u32[]{:S(2)}) %collective-permute-start.2) | collective-permute-done | bytes 786464 | tf_op jit(solution)/shard_map/ppermute | solution.py:34
  40.9 4.6 %collective-permute-start.1 = (bf16[2,128,1536]{1,2,0:T(8,128)(2,1)}, bf16[2,128,1536]{1,2,0:T(8,128)(2,1)}, u32[]{:S(2)}, u32[]{:S(2)}) collective-permute-start(bf16[2,128,1536]{1,2,0:T(8,128)(2,1)} %pad_maximum_fusion.1), channel_id=1, source_target_pairs={{1,0},{2,1},{3,2},{4,3},{5,4},{6,5},{7,6},{8,7},{9,8},{10,9},{11,1... | collective-permute-start | bytes 2359304 | tf_op jit(solution)/shard_map/ppermute | solution.py:24
  45.7 0.7 gather_fusion
  46.5 0.7 gather_fusion.1
  47.5 1.5 %gather_fusion.2 = bf16[2,2,64,1536]{3,2,1,0:T(8,128)(2,1)} fusion(bf16[2,2,64,1536]{3,2,1,0:T(8,128)(2,1)S(1)} %bitcast.105, s32[1024]{0:T(1024)S(1)} %pad_clamp_fusion.5), kind=kCustom, calls=%fused_computation.2.clone | custom fusion | bytes 1572872 | tf_op jit(solution)/shard_map/jit(_take)/gather | solution.py:107
  49.0 0.6 gather_fusion.3
  49.6 1.4 %copy.62 = bf16[2,128,1536]{2,1,0:T(8,128)(2,1)S(1)} copy(bf16[2,128,1536]{1,2,0:T(8,128)(2,1)} %collective-permute-done.4) | data formatting | bytes 1572864 | tf_op jit(solution)/shard_map/ppermute | solution.py:34
  51.0 1.5 %gather_fusion.4 = bf16[2,2,64,1536]{3,2,1,0:T(8,128)(2,1)} fusion(bf16[2,2,64,1536]{3,2,1,0:T(8,128)(2,1)S(1)} %bitcast.107, s32[1024]{0:T(1024)S(1)} %pad_clamp_fusion.3), kind=kCustom, calls=%fused_computation.4.clone | custom fusion | bytes 1572872 | tf_op jit(solution)/shard_map/jit(_take)/gather | solution.py:107
  52.5 1.5 %gather_fusion.5 = bf16[2,2,64,1536]{3,2,1,0:T(8,128)(2,1)} fusion(bf16[2,2,64,1536]{3,2,1,0:T(8,128)(2,1)S(1)} %bitcast.108, s32[1024]{0:T(1024)S(1)} %pad_clamp_fusion.2), kind=kCustom, calls=%fused_computation.5.clone | custom fusion | bytes 1572872 | tf_op jit(solution)/shard_map/jit(_take)/gather | solution.py:107
  54.0 1.4 %copy.63 = bf16[2,128,1536]{2,1,0:T(8,128)(2,1)S(1)} copy(bf16[2,128,1536]{1,2,0:T(8,128)(2,1)} %collective-permute-done.5) | data formatting | bytes 1572864 | tf_op jit(solution)/shard_map/ppermute | solution.py:34
  55.4 1.6 %gather_fusion.6 = bf16[2,2,64,1536]{3,2,1,0:T(8,128)(2,1)} fusion(bf16[2,2,64,1536]{3,2,1,0:T(8,128)(2,1)S(1)} %bitcast.109, s32[1024]{0:T(1024)} %pad_clamp_fusion.1), kind=kCustom, calls=%fused_computation.6.clone | custom fusion | bytes 1572872 | tf_op jit(solution)/shard_map/jit(_take)/gather | solution.py:107
  57.0 1.7 %gather_fusion.7 = bf16[2,2,64,1536]{3,2,1,0:T(8,128)(2,1)} fusion(bf16[2,2,64,1536]{3,2,1,0:T(8,128)(2,1)S(1)} %bitcast.110, s32[1024]{0:T(1024)} %pad_clamp_fusion), kind=kCustom, calls=%fused_computation.7.clone | custom fusion | bytes 1572872 | tf_op jit(solution)/shard_map/jit(_take)/gather | solution.py:107
  59.2 0.7 copy-done.5
  60.8 0.4 copy-done.8
  61.6 2.3 %fusion.30 = (bf16[1,2,8,64,1536]{4,3,0,1,2:T(8,128)(2,1)S(1)}, bf16[1,2,8,64,1536]{4,3,0,1,2:T(8,128)(2,1)}) fusion(bf16[2,2,8,64,1536]{4,3,0,1,2:T(8,128)(2,1)S(1)} %bitcast_dynamic-update-slice_fusion), kind=kLoop, calls=%fused_computation.87 | loop fusion | bytes 12582912 | tf_op jit(solution)/shard_map/slice | solution.py:52
  64.1 3.8 %reshape_squeeze.14 = bf16[2,512,12,128]{3,2,1,0:T(8,128)(2,1)} reshape(bf16[1,2,8,64,1536]{4,3,2,1,0:T(8,128)(2,1)S(1)} %copy.64) | data formatting | bytes 6291456 | tf_op jit(solution)/shard_map/reshape;squeeze | solution.py:52
  68.0 1.8 %pad_maximum_fusion = bf16[2,384,1536]{1,2,0:T(8,128)(2,1)S(1)} fusion(bf16[2,128,1536]{1,2,0:T(8,128)(2,1)} %collective-permute-done.1, bf16[1,128,1536]{1,2,0:T(8,128)(2,1)} %bitcast.117, bf16[1,128,1536]{1,2,0:T(8,128)(2,1)S(1)} %bitcast.115, bf16[2,128,1536]{1,2,0:T(8,128)(2,1)} %collective-permute-done), kind=kLoop, calls=%fused_computation.19 | loop fusion | flops 9437184 | bytes 4718592 | tf_op jit(solution)/shard_map/concatenate | solution.py:20
  70.1 1.9 %copy-done.1 = bf16[2,512,12,128]{3,2,1,0:T(8,128)(2,1)S(1)} copy-done((bf16[2,512,12,128]{3,2,1,0:T(8,128)(2,1)S(1)}, bf16[2,512,12,128]{3,2,1,0:T(8,128)(2,1)}, u32[]{:S(2)}) %copy-start.1) | copy-done | bytes 3145752
  72.1 3.8 %bitcast_reduce_fusion = (f32[2,12,64]{2,1,0:T(8,128)S(1)}, f32[2,12,512,64]{2,3,1,0:T(8,128)}) fusion(pred[512]{0:T(512)(128)(4,1)S(1)} %copy-done.24, bf16[2,64,12,128]{3,2,1,0:T(8,128)(2,1)S(1)} %copy-done.10, bf16[2,512,12,128]{3,2,1,0:T(8,128)(2,1)S(1)} %copy-done.1), kind=kOutput, calls=%fused_computation.9 | convolution fusion | flops 203684352 | bytes 6691328 | tf_op jit(solution)/shard_map/bqhd,bkhd->bhqk/dot_general | solution.py:60
  75.9 0.5 fusion.32
  76.9 1.4 %fusion.8 = f32[2,12,64]{2,0,1:T(2,128)} fusion(f32[12,384,2,64]{1,3,2,0:T(8,128)S(1)} %bitcast.101, f32[2,12,64]{2,0,1:T(2,128)S(1)} %copy_maximum_fusion, pred[384]{0:T(512)(128)(4,1)S(1)} %copy-done.21), kind=kLoop, calls=%fused_computation.24 | loop fusion | flops 2357760 | bytes 2371968 | tf_op jit(solution)/shard_map/reduce_sum | solution.py:67
  78.3 0.6 copy.70
  78.9 2.0 %copy.69 = bf16[1,2,8,64,1536]{4,3,2,1,0:T(8,128)(2,1)} copy(bf16[1,2,8,64,1536]{4,3,0,1,2:T(8,128)(2,1)S(1)} %copy-done) | data formatting | bytes 6291456 | tf_op jit(solution)/shard_map/slice | solution.py:53
  80.8 6.9 %reshape_squeeze.15 = bf16[2,512,12,128]{3,2,1,0:T(8,128)(2,1)} reshape(bf16[1,2,8,64,1536]{4,3,2,1,0:T(8,128)(2,1)} %copy.69) | data formatting | bytes 6291456 | tf_op jit(solution)/shard_map/reshape;squeeze | solution.py:53
  87.7 3.0 %fusion.5 = (f32[2,12,64]{2,1,0:T(8,128)S(1)}, bf16[2,12,64,512]{3,2,1,0:T(8,128)(2,1)S(1)}) fusion(f32[2,12,512,64]{2,3,1,0:T(8,128)} %get-tuple-element.21, f32[2,12,64]{2,1,0:T(8,128)} %copy.70, pred[512]{0:T(512)(128)(4,1)} %reshape.45), kind=kLoop, calls=%fused_computation.17 | loop fusion | flops 3930624 | bytes 4731392 | tf_op jit(solution)/shard_map/reduce_sum | solution.py:67
  90.9 1.8 %fusion.11 = f32[2,64,12,128]{3,1,0,2:T(8,128)S(1)} fusion(bf16[2,512,12,128]{3,2,1,0:T(8,128)(2,1)S(1)} %copy-done.2, bf16[2,12,64,512]{3,2,1,0:T(8,128)(2,1)S(1)} %get-tuple-element.17), kind=kOutput, calls=%fused_computation.27 | convolution fusion | flops 201326592 | bytes 5505024 | tf_op jit(solution)/shard_map/bhqk,bkhd->bqhd/dot_general | solution.py:74
  92.7 0.9 fusion.18
  94.0 1.6 %convolution_convert_fusion = bf16[128,1536]{1,0:T(8,128)(2,1)} fusion(bf16[1536,1536]{1,0:T(8,128)(2,1)S(1)} %bitcast.112, bf16[16,8,12,128]{3,2,1,0:T(8,128)(2,1)S(1)} %bitcast.118), kind=kOutput, calls=%fused_computation.16 | convolution fusion | flops 604176384 | bytes 5505024 | tf_op jit(solution)/shard_map/dot_general | solution.py:85
  (86 shorter events, 4.7 us)
Async XLA Ops:
  0.0 19.9 %copy-start.13 = (s32[2,8]{1,0:T(2,128)S(1)}, s32[2,8]{1,0:T(2,128)}, u32[]{:S(2)}) copy-start(s32[2,8]{1,0:T(2,128)} %param.10) | copy-start | bytes 196
  0.0 24.7 %copy-start.12 = (bf16[128,1536]{1,0:T(8,128)(2,1)S(1)}, bf16[128,1536]{1,0:T(8,128)(2,1)}, u32[]{:S(2)}) copy-start(bf16[128,1536]{1,0:T(8,128)(2,1)} %param.7) | copy-start | bytes 1179652
  2.5 38.4 %copy-start.3 = (bf16[128,1536]{0,1:T(8,128)(2,1)}, bf16[128,1536]{0,1:T(8,128)(2,1)S(1)}, u32[]{:S(2)}) copy-start(bf16[128,1536]{0,1:T(8,128)(2,1)S(1)} %copy.57) | copy-start | bytes 1179652
  3.5 37.4 %collective-permute-start.2 = (bf16[2,128,1536]{1,2,0:T(8,128)(2,1)}, bf16[2,128,1536]{1,2,0:T(8,128)(2,1)S(1)}, u32[]{:S(2)}, u32[]{:S(2)}) collective-permute-start(bf16[2,128,1536]{1,2,0:T(8,128)(2,1)} %pad_maximum_fusion.1), channel_id=1, source_target_pairs={{0,2},{1,3},{2,4},{3,5},{4,6},{5,7},{6,8},{7,9},{8,10},{9,11},{10,... | collective-permute-start | bytes 2359304 | tf_op jit(solution)/shard_map/ppermute | solution.py:34
  6.7 40.5 %collective-permute-start.3 = (bf16[2,128,1536]{1,2,0:T(8,128)(2,1)}, bf16[2,128,1536]{1,2,0:T(8,128)(2,1)S(1)}, u32[]{:S(2)}, u32[]{:S(2)}) collective-permute-start(bf16[2,128,1536]{1,2,0:T(8,128)(2,1)} %pad_maximum_fusion.1), channel_id=1, source_target_pairs={{0,4},{1,5},{2,6},{3,7},{4,8},{5,9},{6,10},{7,11},{8,12},{9,13},{1... | collective-permute-start | bytes 2359304 | tf_op jit(solution)/shard_map/ppermute | solution.py:34
  9.9 39.7 %collective-permute-start.4 = (bf16[2,128,1536]{1,2,0:T(8,128)(2,1)}, bf16[2,128,1536]{1,2,0:T(8,128)(2,1)}, u32[]{:S(2)}, u32[]{:S(2)}) collective-permute-start(bf16[2,128,1536]{1,2,0:T(8,128)(2,1)} %pad_maximum_fusion.1), channel_id=1, source_target_pairs={{2,0},{3,1},{4,2},{5,3},{6,4},{7,5},{8,6},{9,7},{10,8},{11,9},{12,... | collective-permute-start | bytes 2359304 | tf_op jit(solution)/shard_map/ppermute | solution.py:34
  12.0 42.0 %collective-permute-start.5 = (bf16[2,128,1536]{1,2,0:T(8,128)(2,1)}, bf16[2,128,1536]{1,2,0:T(8,128)(2,1)}, u32[]{:S(2)}, u32[]{:S(2)}) collective-permute-start(bf16[2,128,1536]{1,2,0:T(8,128)(2,1)} %pad_maximum_fusion.1), channel_id=1, source_target_pairs={{4,0},{5,1},{6,2},{7,3},{8,4},{9,5},{10,6},{11,7},{12,8},{13,9},{1... | collective-permute-start | bytes 2359304 | tf_op jit(solution)/shard_map/ppermute | solution.py:34
  14.1 53.8 %collective-permute-start = (bf16[2,128,1536]{1,2,0:T(8,128)(2,1)}, bf16[2,128,1536]{1,2,0:T(8,128)(2,1)}, u32[]{:S(2)}, u32[]{:S(2)}) collective-permute-start(bf16[2,128,1536]{1,2,0:T(8,128)(2,1)} %pad_maximum_fusion.1), channel_id=1, source_target_pairs={{0,1},{1,2},{2,3},{3,4},{4,5},{5,6},{6,7},{7,8},{8,9},{9,10},{10,1... | collective-permute-start | bytes 2359304 | tf_op jit(solution)/shard_map/ppermute | solution.py:22
  24.9 15.9 %copy-start.9 = (bf16[2,64,12,128]{3,2,1,0:T(8,128)(2,1)}, bf16[2,64,12,128]{3,2,1,0:T(8,128)(2,1)S(1)}, u32[]{:S(2)}) copy-start(bf16[2,64,12,128]{3,2,1,0:T(8,128)(2,1)S(1)} %reshape.44) | copy-start | bytes 1179652
  40.9 27.1 %collective-permute-start.1 = (bf16[2,128,1536]{1,2,0:T(8,128)(2,1)}, bf16[2,128,1536]{1,2,0:T(8,128)(2,1)}, u32[]{:S(2)}, u32[]{:S(2)}) collective-permute-start(bf16[2,128,1536]{1,2,0:T(8,128)(2,1)} %pad_maximum_fusion.1), channel_id=1, source_target_pairs={{1,0},{2,1},{3,2},{4,3},{5,4},{6,5},{7,6},{8,7},{9,8},{10,9},{11,1... | collective-permute-start | bytes 2359304 | tf_op jit(solution)/shard_map/ppermute | solution.py:24
  52.5 6.3 %copy-start.23 = (pred[2]{0:T(512)(128)(4,1)S(1)}, pred[2]{0:T(512)(128)(4,1)}, u32[]{:S(2)}) copy-start(pred[2]{0:T(512)(128)(4,1)} %compare_and_fusion.7) | copy-start | bytes 10
  54.0 5.0 %copy-start.20 = (pred[2]{0:T(512)(128)(4,1)S(1)}, pred[2]{0:T(512)(128)(4,1)}, u32[]{:S(2)}) copy-start(pred[2]{0:T(512)(128)(4,1)} %get-tuple-element.35) | copy-start | bytes 10
  55.4 3.8 %copy-start.19 = (pred[2]{0:T(512)(128)(4,1)S(1)}, pred[2]{0:T(512)(128)(4,1)}, u32[]{:S(2)}) copy-start(pred[2]{0:T(512)(128)(4,1)} %get-tuple-element.34) | copy-start | bytes 10
  57.0 3.1 %copy-start.18 = (pred[2]{0:T(512)(128)(4,1)S(1)}, pred[2]{0:T(512)(128)(4,1)}, u32[]{:S(2)}) copy-start(pred[2]{0:T(512)(128)(4,1)} %get-tuple-element.33) | copy-start | bytes 10
  58.8 1.1 %copy-start.5 = (bf16[2,2,64,1536]{3,2,1,0:T(8,128)(2,1)S(1)}, bf16[2,2,64,1536]{3,2,1,0:T(8,128)(2,1)}, u32[]{:S(2)}) copy-start(bf16[2,2,64,1536]{3,2,1,0:T(8,128)(2,1)} %gather_fusion.2) | copy-start | bytes 2359300
  58.8 1.6 %copy-start.7 = (bf16[2,2,64,1536]{3,2,1,0:T(8,128)(2,1)S(1)}, bf16[2,2,64,1536]{3,2,1,0:T(8,128)(2,1)}, u32[]{:S(2)}) copy-start(bf16[2,2,64,1536]{3,2,1,0:T(8,128)(2,1)} %gather_fusion.4) | copy-start | bytes 2359300
  58.8 1.6 %copy-start.17 = (pred[2]{0:T(512)(128)(4,1)S(1)}, pred[2]{0:T(512)(128)(4,1)}, u32[]{:S(2)}) copy-start(pred[2]{0:T(512)(128)(4,1)} %get-tuple-element.32) | copy-start | bytes 10
  59.0 1.6 %copy-start.4 = (bf16[2,2,64,1536]{3,2,1,0:T(8,128)(2,1)S(1)}, bf16[2,2,64,1536]{3,2,1,0:T(8,128)(2,1)}, u32[]{:S(2)}) copy-start(bf16[2,2,64,1536]{3,2,1,0:T(8,128)(2,1)} %gather_fusion.5) | copy-start | bytes 2359300
  59.0 1.6 %copy-start.16 = (pred[2]{0:T(512)(128)(4,1)S(1)}, pred[2]{0:T(512)(128)(4,1)}, u32[]{:S(2)}) copy-start(pred[2]{0:T(512)(128)(4,1)} %get-tuple-element.31) | copy-start | bytes 10
  59.9 1.3 %copy-start.8 = (bf16[2,2,64,1536]{3,2,1,0:T(8,128)(2,1)S(1)}, bf16[2,2,64,1536]{3,2,1,0:T(8,128)(2,1)}, u32[]{:S(2)}) copy-start(bf16[2,2,64,1536]{3,2,1,0:T(8,128)(2,1)} %gather_fusion.6) | copy-start | bytes 2359300
  59.9 1.3 %copy-start.15 = (pred[2]{0:T(512)(128)(4,1)S(1)}, pred[2]{0:T(512)(128)(4,1)}, u32[]{:S(2)}) copy-start(pred[2]{0:T(512)(128)(4,1)} %get-tuple-element.30) | copy-start | bytes 10
  60.1 1.2 %copy-start.6 = (bf16[2,2,64,1536]{3,2,1,0:T(8,128)(2,1)S(1)}, bf16[2,2,64,1536]{3,2,1,0:T(8,128)(2,1)}, u32[]{:S(2)}) copy-start(bf16[2,2,64,1536]{3,2,1,0:T(8,128)(2,1)} %gather_fusion.7) | copy-start | bytes 2359300
  60.1 1.2 %copy-start.22 = (pred[2]{0:T(512)(128)(4,1)S(1)}, pred[2]{0:T(512)(128)(4,1)}, u32[]{:S(2)}) copy-start(pred[2]{0:T(512)(128)(4,1)} %compare_and_fusion) | copy-start | bytes 10
  68.0 2.1 %copy-start.24 = (pred[512]{0:T(512)(128)(4,1)S(1)}, pred[512]{0:T(512)(128)(4,1)}, u32[]{:S(2)}) copy-start(pred[512]{0:T(512)(128)(4,1)} %reshape.45) | copy-start | bytes 1540
  69.8 2.2 %copy-start.1 = (bf16[2,512,12,128]{3,2,1,0:T(8,128)(2,1)S(1)}, bf16[2,512,12,128]{3,2,1,0:T(8,128)(2,1)}, u32[]{:S(2)}) copy-start(bf16[2,512,12,128]{3,2,1,0:T(8,128)(2,1)} %reshape_squeeze.14) | copy-start | bytes 9437188
  69.8 2.3 %copy-start.10 = (bf16[2,64,12,128]{3,2,1,0:T(8,128)(2,1)S(1)}, bf16[2,64,12,128]{3,2,1,0:T(8,128)(2,1)}, u32[]{:S(2)}) copy-start(bf16[2,64,12,128]{3,2,1,0:T(8,128)(2,1)} %copy-done.9) | copy-start | bytes 1179652
  72.1 3.8 %copy-start.11 = (bf16[2,64,12,128]{3,1,0,2:T(8,128)(2,1)S(1)}, bf16[2,64,12,128]{3,1,0,2:T(8,128)(2,1)}, u32[]{:S(2)}) copy-start(bf16[2,64,12,128]{3,1,0,2:T(8,128)(2,1)} %copy.59) | copy-start | bytes 1179652
  75.9 0.6 copy-start.21
  76.4 2.5 %copy-start = (bf16[1,2,8,64,1536]{4,3,0,1,2:T(8,128)(2,1)S(1)}, bf16[1,2,8,64,1536]{4,3,0,1,2:T(8,128)(2,1)}, u32[]{:S(2)}) copy-start(bf16[1,2,8,64,1536]{4,3,0,1,2:T(8,128)(2,1)} %get-tuple-element.15) | copy-start | bytes 9437188
  87.7 3.0 %copy-start.14 = (f32[2,12,64]{2,0,1:T(2,128)S(1)}, f32[2,12,64]{2,0,1:T(2,128)}, u32[]{:S(2)}) copy-start(f32[2,12,64]{2,0,1:T(2,128)} %fusion.8) | copy-start | bytes 18436
  87.7 3.2 %copy-start.2 = (bf16[2,512,12,128]{3,2,1,0:T(8,128)(2,1)S(1)}, bf16[2,512,12,128]{3,2,1,0:T(8,128)(2,1)}, u32[]{:S(2)}) copy-start(bf16[2,512,12,128]{3,2,1,0:T(8,128)(2,1)} %reshape_squeeze.15) | copy-start | bytes 9437188
  90.9 3.1 %slice-start = ((s8[4718592]{0:T(1024)(128)(4,1)}), s8[4194304]{0:T(1024)(128)(4,1)S(1)}, s32[]{:S(2)}) async-start(s8[4718592]{0:T(1024)(128)(4,1)} %bitcast.111), calls=%async_computation | async-start | bytes 8388608
  92.7 1.3 %slice-start.1 = ((s8[4718592]{0:T(1024)(128)(4,1)}), s8[524288]{0:T(1024)(128)(4,1)S(1)}, s32[]{:S(2)}) async-start(s8[4718592]{0:T(1024)(128)(4,1)} %bitcast.111), calls=%async_computation.1 | async-start | bytes 1048576
where the time goes:
time: 96.1 us; the launch traced here: 95.5 us
  local copies, waits for them, and re-layouts  38.3 us (40%)
  starting transfers between devices  20.9 us (22%)
  other arithmetic  14.5 us (15%)
  waiting for transfers between devices  12.8 us (13%)
  matrix products  8.6 us (9%)
    ppermute x4, waiting for transfers between devices, shifted(): return lax.ppermute(block, axis, route)  12.8 us
    ppermute x4, starting transfers between devices, shifted(): return lax.ppermute(block, axis, route)  10.6 us
    gather x8, local copies, waits for them, and re-layouts, body(): chosen_list.append(jnp.take(source, far_picks[:, column], axis=1))  9.84 us
    another operation x1, local copies, waits for them, and re-layouts, attend(): far_values = far_pair[1].reshape(blocks, -1, HEADS, HEAD_DIM)  6.86 us
    unnamed x56, local copies, waits for them, and re-layouts  5.89 us
    ppermute x1, starting transfers between devices, padded(): lax.ppermute(tail, axis, [(i, (i + 1) % count) for i in range(ends)])  5.73 us
    ppermute x1, starting transfers between devices, padded(): lax.ppermute(head, axis, [((i + 1) % count, i) for i in range(ends)])  4.56 us
    reduce_sum x2, other arithmetic, attend(): total = jnp.sum(near_exp, -1) + jnp.sum(far_exp, -1)  4.42 us
  transfers between devices with their start and end apart: 6, of which 1 were waited for; matrix products, arithmetic and copies ran while one was open for 31% of the time, Pallas kernels for 0%

commit v1 on v0

v1 whole, which is shorter than its diff:
```python
import functools
import math

import jax
import jax.numpy as jnp
from jax import lax
from jax.experimental import pallas as pl
from jax.experimental.pallas import tpu as pltpu
from jax.sharding import PartitionSpec as P

HEADS = 12
HEAD_DIM = 128
BLK = 64
NEG = -1e30
EXP_SCALE = HEAD_DIM ** (-0.5) * math.log2(math.e)
OWN, SIB, YN, ZP, ZM, DG, XF = range(7)
MESH = pl.DeviceIdType.MESH


def kernel(
    devices,
    picks,
    q_hbm,
    k_hbm,
    v_hbm,
    out,
    qv,
    kbuf,
    vbuf,
    mult,
    top,
    tot,
    acc,
    load_sem,
    send_sem,
    recv_sem,
):
    rows = q_hbm.shape[0]
    half = rows // 2
    chips = devices // 2
    p = lax.axis_index("tm")
    chip = p // 2
    core = p % 2
    even = chip % 2 == 0
    step = jnp.where(even, 1, -1)
    has_p = (chip + 2 * step >= 0) & (chip + 2 * step < chips)
    has_m = (chip - 2 * step >= 0) & (chip - 2 * step < chips)
    gives_y = (core + chip) % 2 == 0
    gives_d = jnp.logical_not(gives_y)

    sib = p + 1 - 2 * core
    y_dev = p + 2 * step
    zp_dev = p + 4 * step
    zm_dev = p - 4 * step

    def slot(buf, index):
        return buf.at[pl.ds(index * rows, rows)]

    def part(buf, index, which):
        return buf.at[pl.ds(index * rows + which * half, half)]

    def remote(src, dst, number, kv, dev):
        return pltpu.make_async_remote_copy(
            src_ref=src,
            dst_ref=dst,
            send_sem=send_sem.at[number, kv],
            recv_sem=recv_sem.at[number, kv],
            device_id={"tm": dev},
            device_id_type=MESH,
        )

    bufs = (kbuf, vbuf)
    hbms = (k_hbm, v_hbm)

    def to_sib(kv):
        return remote(hbms[kv], slot(bufs[kv], SIB), 0, kv, sib)

    def to_y(kv):
        return remote(hbms[kv], slot(bufs[kv], YN), 1, kv, y_dev)

    def to_zp(kv):
        return remote(hbms[kv], slot(bufs[kv], ZM), 2, kv, zp_dev)

    def to_zm(kv):
        return remote(hbms[kv], slot(bufs[kv], ZP), 3, kv, zm_dev)

    def relay_y(kv):
        return remote(part(bufs[kv], YN, 0), part(bufs[kv], DG, 0), 4, kv, zp_dev)

    def relay_z(kv):
        return remote(part(bufs[kv], ZP, 1), part(bufs[kv], DG, 1), 5, kv, y_dev)

    def hand_y(kv):
        return remote(slot(bufs[kv], YN), slot(bufs[kv], XF), 6, kv, sib)

    def hand_d(kv):
        return remote(slot(bufs[kv], DG), slot(bufs[kv], XF), 6, kv, sib)

    loads = [
        pltpu.make_async_copy(q_hbm, qv, load_sem.at[0]),
        pltpu.make_async_copy(k_hbm, slot(kbuf, OWN), load_sem.at[1]),
        pltpu.make_async_copy(v_hbm, slot(vbuf, OWN), load_sem.at[2]),
    ]
    for load in loads:
        load.start()

    barrier = pltpu.get_barrier_semaphore()

    def greet(dev):
        pl.semaphore_signal(barrier, inc=1, device_id={"tm": dev}, device_id_type=MESH)

    greet(sib)
    greet(y_dev)

    @pl.when(has_p)
    def _():
        greet(zp_dev)

    @pl.when(has_m)
    def _():
        greet(zm_dev)

    pl.semaphore_wait(barrier, 2 + jnp.where(has_p, 1, 0) + jnp.where(has_m, 1, 0))

    for kv in range(2):
        to_y(kv).start()

        @pl.when(has_p)
        def _():
            to_zp(kv).start()

        @pl.when(has_m)
        def _():
            to_zm(kv).start()

        to_sib(kv).start()

    ints = jnp.int32
    row_first = lax.broadcasted_iota(ints, (rows, rows), 0) < BLK
    col_first = lax.broadcasted_iota(ints, (rows, rows), 1) < BLK

    def fill(index, up, down, valid):
        one = jnp.where(valid, 1, 0)
        seconds = [
            jnp.where(even, picks[b, up] + picks[b, up + 1], picks[b, down] + picks[b, down + 1])
            for b in range(2)
        ]
        cells = [[((2 - n) * one).astype(jnp.float32), (n * one).astype(jnp.float32)] for n in seconds]
        mult[index] = jnp.where(
            row_first,
            jnp.where(col_first, cells[0][0], cells[0][1]),
            jnp.where(col_first, cells[1][0], cells[1][1]),
        )

    fill(0, 4, 0, True)
    fill(1, 6, 2, has_p)
    fill(2, 2, 6, has_m)
    fill(3, 0, 4, has_m)
    x_valid = gives_d | has_m
    mult[4] = jnp.full((rows, rows), jnp.where(x_valid, 1.0, 0.0), jnp.float32)

    @pl.when(jnp.logical_not(has_p))
    def _():
        vbuf[ZP * rows : (ZP + 1) * rows] = jnp.zeros((rows, vbuf.shape[1]), vbuf.dtype)

    @pl.when(jnp.logical_not(has_m))
    def _():
        vbuf[ZM * rows : (DG + 1) * rows] = jnp.zeros((2 * rows, vbuf.shape[1]), vbuf.dtype)

    @pl.when(jnp.logical_not(x_valid))
    def _():
        vbuf[XF * rows : (XF + 1) * rows] = jnp.zeros((rows, vbuf.shape[1]), vbuf.dtype)

    def head_group(head, first_slot, factors, first, last):
        columns = pl.ds(pl.multiple_of(head * HEAD_DIM, HEAD_DIM), HEAD_DIM)
        count = len(factors)
        slots = pl.ds(first_slot * rows, count * rows)
        scores = lax.dot_general(
            qv[:, columns],
            kbuf[slots, columns],
            (((1,), (1,)), ((), ())),
            preferred_element_type=jnp.float32,
        )
        pieces = []
        for i, factor in enumerate(factors):
            piece = scores[:, i * rows : (i + 1) * rows]
            if factor is not None:
                piece = jnp.where(mult[factor] > 0, piece, NEG)
            pieces.append(piece)
        high = functools.reduce(jnp.maximum, pieces)
        high = jnp.broadcast_to(jnp.max(high, axis=1, keepdims=True), high.shape)
        if not first:
            before = top[head]
            high = jnp.maximum(high, before)
            fade = jnp.exp2((before - high) * EXP_SCALE)
        weights = []
        for piece, factor in zip(pieces, factors):
            weight = jnp.exp2((piece - high) * EXP_SCALE)
            if factor is not None:
                weight = weight * mult[factor]
            weights.append(weight)
        summed = functools.reduce(jnp.add, weights)
        summed = jnp.broadcast_to(jnp.sum(summed, axis=1, keepdims=True), summed.shape)
        mixed = jnp.dot(
            jnp.concatenate([w.astype(jnp.bfloat16) for w in weights], axis=1),
            vbuf[slots, columns],
            preferred_element_type=jnp.float32,
        )
        if not first:
            summed = summed + tot[head] * fade
            mixed = mixed + acc[head] * fade
        if last:
            out[:, columns] = (mixed / summed).astype(out.dtype)
        else:
            top[head] = high
            tot[head] = summed
            acc[head] = mixed

    def group(first_slot, factors, first, last, unroll):
        def body(index, carry):
            for u in range(unroll):
                head_group(index * unroll + u, first_slot, factors, first, last)
            return carry

        if unroll == HEADS:
            body(0, 0)
        else:
            lax.fori_loop(0, HEADS // unroll, body, 0)

    for load in loads:
        load.wait()
    for kv in range(2):
        to_sib(kv).wait_recv()
    group(OWN, (None, None), True, False, 4)

    for kv in range(2):
        to_y(kv).wait_recv()

        @pl.when(has_p)
        def _():
            relay_y(kv).start()

        @pl.when(gives_y)
        def _():
            hand_y(kv).start()

        @pl.when(has_p)
        def _():
            to_zm(kv).wait_recv()
            relay_z(kv).start()

    @pl.when(has_m)
    def _():
        for kv in range(2):
            to_zp(kv).wait_recv()

    group(YN, (0, 1, 2), False, False, 4)

    for kv in range(2):

        @pl.when(has_m)
        def _():
            relay_y(kv).wait_recv()
            relay_z(kv).wait_recv()

        @pl.when(has_m & gives_d)
        def _():
            hand_d(kv).start()

    for kv in range(2):

        @pl.when(x_valid)
        def _():
            hand_y(kv).wait_recv()

    group(DG, (3, 4), False, True, 4)

    for kv in range(2):
        to_sib(kv).wait_send()
        to_y(kv).wait_send()

        @pl.when(has_p)
        def _():
            to_zp(kv).wait_send()
            relay_y(kv).wait_send()
            relay_z(kv).wait_send()

        @pl.when(has_m)
        def _():
            to_zm(kv).wait_send()

        @pl.when(gives_y | has_m)
        def _():
            hand_y(kv).wait_send()


def attention(devices, queries, keys, values, far_picks):
    rows, width = queries.shape
    anywhere = pl.BlockSpec(memory_space=pl.ANY)
    return pl.pallas_call(
        functools.partial(kernel, devices),
        out_shape=jax.ShapeDtypeStruct((rows, width), jnp.bfloat16),
        in_specs=[pl.BlockSpec(memory_space=pltpu.SMEM), anywhere, anywhere, anywhere],
        out_specs=pl.BlockSpec(memory_space=pltpu.VMEM),
        scratch_shapes=[
            pltpu.VMEM((rows, width), jnp.bfloat16),
            pltpu.VMEM((7 * rows, width), jnp.bfloat16),
            pltpu.VMEM((7 * rows, width), jnp.bfloat16),
            pltpu.VMEM((5, rows, rows), jnp.float32),
            pltpu.VMEM((HEADS, rows, HEAD_DIM), jnp.float32),
            pltpu.VMEM((HEADS, rows, HEAD_DIM), jnp.float32),
            pltpu.VMEM((HEADS, rows, HEAD_DIM), jnp.float32),
            pltpu.SemaphoreType.DMA((3,)),
            pltpu.SemaphoreType.DMA((7, 2)),
            pltpu.SemaphoreType.DMA((7, 2)),
        ],
        compiler_params=pltpu.CompilerParams(
            collective_id=0, has_side_effects=True, vmem_limit_bytes=24 * 1024 * 1024
        ),
        name="relay_attention",
    )(far_picks, queries, keys, values)


def solution(mesh):
    devices = mesh.shape["tm"]

    def body(queries, keys, values, far_picks, out_weight):
        attended = attention(devices, queries, keys, values, far_picks)
        return jnp.dot(attended, out_weight, preferred_element_type=jnp.float32).astype(jnp.bfloat16)

    placed = (
        P(("vid", "tm"), None),
        P(("vid", "tm"), None),
        P(("vid", "tm"), None),
        P(("vid", "tm"), None),
        P(),
    )
    return jax.shard_map(
        body, mesh=mesh, in_specs=placed, out_specs=P(("vid", "tm"), None), check_vma=False
    )
```

time: 96.1 us -> 42.2 us (0.44)
  local copies, waits for them, and re-layouts: 38.3 us -> 3.66 us
  Pallas kernels: 0 us -> 34.3 us
  starting transfers between devices: 20.9 us -> 0 us
  other arithmetic: 14.5 us -> 0 us
  waiting for transfers between devices: 12.8 us -> 0 us
  matrix products: 8.6 us -> 3.89 us
    pallas_call x0 -> x1, Pallas kernels: none -> 34.3 us  [attention(): pl.pallas_call(functools.partial(kernel, devices), out_shape=jax.ShapeDty...]
    ppermute x6 -> x0, starting transfers between devices: 20.9 us -> none  [the longest x4 10.6 us: shifted(): return lax.ppermute(block, axis, route)]
    ppermute x6 -> x0, waiting for transfers between devices: 12.8 us -> none  [the longest x4 12.8 us: shifted(): return lax.ppermute(block, axis, route)]
    another operation x3 -> x0, local copies, waits for them, and re-layouts: 10.8 us -> none  [the longest x1 6.86 us: attend(): far_values = far_pair[1].reshape(blocks, -1, HEADS, HEAD_DIM)]
    gather x8 -> x0, local copies, waits for them, and re-layouts: 9.84 us -> none  [body(): chosen_list.append(jnp.take(source, far_picks[:, column], axis=1))]
    slice x5 -> x0, local copies, waits for them, and re-layouts: 5.02 us -> none  [the longest x2 2.54 us: attend(): far_keys = far_pair[0].reshape(blocks, -1, HEADS, HEAD_DIM)]
    reduce_sum x2 -> x0, other arithmetic: 4.42 us -> none  [attend(): total = jnp.sum(near_exp, -1) + jnp.sum(far_exp, -1)]
    dot_general x4 -> x1, matrix products: 8.13 us -> 3.89 us  [body(): jnp.dot(attended, out_weight, preferred_element_type=jnp.float32)]
  transfers between devices with their start and end apart: 6 -> 0, of which waited for: 1 -> 0; matrix products, arithmetic and copies ran while one was open for 31% -> 0% of each run, Pallas kernels for 0% -> 0%
where the time goes in v1:
time: 42.2 us; the launch traced here: 41.9 us
  Pallas kernels  34.3 us (81%)
  matrix products  3.89 us (9%)
  local copies, waits for them, and re-layouts  3.66 us (9%)
    pallas_call x1, Pallas kernels, attention(): pl.pallas_call(functools.partial(kernel, devices), out_shape=jax.ShapeDty...  34.3 us
    dot_general x1, matrix products, body(): jnp.dot(attended, out_weight, preferred_element_type=jnp.float32)  3.89 us
    unnamed x8, local copies, waits for them, and re-layouts  3.66 us

profile of v1, /device:TPU:15, one launch (start us, length us, event | category | flops | bytes accessed | tf_op | source)
XLA Modules:
  0.0 41.9 jit_solution(8181989893557804403)
XLA Ops:
  0.0 0.0 copy-start
  0.0 1.0 %copy-done = bf16[128,1536]{1,0:T(8,128)(2,1)S(1)} copy-done((bf16[128,1536]{1,0:T(8,128)(2,1)S(1)}, bf16[128,1536]{1,0:T(8,128)(2,1)}, u32[]{:S(2)}) %copy-start) | copy-done | bytes 393240
  1.0 0.0 copy-start.1
  1.0 1.0 %copy-done.1 = bf16[128,1536]{1,0:T(8,128)(2,1)S(1)} copy-done((bf16[128,1536]{1,0:T(8,128)(2,1)S(1)}, bf16[128,1536]{1,0:T(8,128)(2,1)}, u32[]{:S(2)}) %copy-start.1) | copy-done | bytes 393240
  2.0 0.0 copy-start.2
  2.0 1.0 %copy-done.2 = bf16[128,1536]{1,0:T(8,128)(2,1)S(1)} copy-done((bf16[128,1536]{1,0:T(8,128)(2,1)S(1)}, bf16[128,1536]{1,0:T(8,128)(2,1)}, u32[]{:S(2)}) %copy-start.2) | copy-done | bytes 393240
  3.0 0.0 copy-start.3
  3.0 0.7 %copy-done.3 = s32[2,8]{1,0:T(2,128)S(1)} copy-done((s32[2,8]{1,0:T(2,128)S(1)}, s32[2,8]{1,0:T(2,128)}, u32[]{:S(2)}) %copy-start.3) | copy-done | bytes 88
  3.7 34.3 %relay_attention.1 = bf16[128,1536]{1,0:T(8,128)(2,1)S(1)} custom-call(s32[2,8]{1,0:T(2,128)S(1)} %copy-done.3, bf16[128,1536]{1,0:T(8,128)(2,1)S(1)} %copy-done, bf16[128,1536]{1,0:T(8,128)(2,1)S(1)} %copy-done.1, bf16[128,1536]{1,0:T(8,128)(2,1)S(1)} %copy-done.2), custom_call_target="tpu_custom_call" | custom-call | tf_op jit(solution)/shard_map/relay_attention/pallas_call | solution.py:300
  38.0 3.9 %convolution_convert_fusion = bf16[128,1536]{1,0:T(8,128)(2,1)} fusion(bf16[128,1536]{1,0:T(8,128)(2,1)S(1)} %relay_attention.1, bf16[1536,1536]{1,0:T(8,128)(2,1)} %param.9), kind=kOutput, calls=%fused_computation | convolution fusion | flops 604176384 | bytes 5505024 | tf_op jit(solution)/shard_map/dot_general | solution.py:329
Async XLA Ops:
  0.0 1.0 %copy-start = (bf16[128,1536]{1,0:T(8,128)(2,1)S(1)}, bf16[128,1536]{1,0:T(8,128)(2,1)}, u32[]{:S(2)}) copy-start(bf16[128,1536]{1,0:T(8,128)(2,1)} %q_hbm.1) | copy-start | bytes 1179652
  1.0 1.0 %copy-start.1 = (bf16[128,1536]{1,0:T(8,128)(2,1)S(1)}, bf16[128,1536]{1,0:T(8,128)(2,1)}, u32[]{:S(2)}) copy-start(bf16[128,1536]{1,0:T(8,128)(2,1)} %k_hbm.1) | copy-start | bytes 1179652
  2.0 1.0 %copy-start.2 = (bf16[128,1536]{1,0:T(8,128)(2,1)S(1)}, bf16[128,1536]{1,0:T(8,128)(2,1)}, u32[]{:S(2)}) copy-start(bf16[128,1536]{1,0:T(8,128)(2,1)} %v_hbm.1) | copy-start | bytes 1179652
  3.0 0.7 %copy-start.3 = (s32[2,8]{1,0:T(2,128)S(1)}, s32[2,8]{1,0:T(2,128)}, u32[]{:S(2)}) copy-start(s32[2,8]{1,0:T(2,128)} %picks.1) | copy-start | bytes 196

commit v2 on v1

--- a/solution.py
+++ b/solution.py
@@ -19,12 +19,17 @@
 
 def kernel(
     devices,
-    picks,
+    picks_hbm,
     q_hbm,
     k_hbm,
     v_hbm,
+    w_hbm,
     out,
+    picks,
     qv,
+    wv,
+    late,
+    mixed_heads,
     kbuf,
     vbuf,
     mult,
@@ -90,12 +95,15 @@
     def relay_z(kv):
         return remote(part(bufs[kv], ZP, 1), part(bufs[kv], DG, 1), 5, kv, y_dev)
 
-    def hand_y(kv):
-        return remote(slot(bufs[kv], YN), slot(bufs[kv], XF), 6, kv, sib)
-
-    def hand_d(kv):
-        return remote(slot(bufs[kv], DG), slot(bufs[kv], XF), 6, kv, sib)
-
+    def hand_y(kv, which):
+        return remote(part(bufs[kv], YN, which), part(bufs[kv], XF, which), 6 + which, kv, sib)
+
+    def hand_d(kv, which):
+        return remote(part(bufs[kv], DG, which), part(bufs[kv], XF, which), 6 + which, kv, sib)
+
+    load_w = pltpu.make_async_copy(w_hbm, wv, load_sem.at[4])
+    load_picks = pltpu.make_async_copy(picks_hbm, picks, load_sem.at[3])
+    load_picks.start()
     loads = [
         pltpu.make_async_copy(q_hbm, qv, load_sem.at[0]),
         pltpu.make_async_copy(k_hbm, slot(kbuf, OWN), load_sem.at[1]),
@@ -134,6 +142,9 @@
             to_zm(kv).start()
 
         to_sib(kv).start()
+
+    load_w.start()
+    load_picks.wait()
 
     ints = jnp.int32
     row_first = lax.broadcasted_iota(ints, (rows, rows), 0) < BLK
@@ -171,7 +182,7 @@
     def _():
         vbuf[XF * rows : (XF + 1) * rows] = jnp.zeros((rows, vbuf.shape[1]), vbuf.dtype)
 
-    def head_group(head, first_slot, factors, first, last):
+    def head_group(head, first_slot, factors, first, values_later):
         columns = pl.ds(pl.multiple_of(head * HEAD_DIM, HEAD_DIM), HEAD_DIM)
         count = len(factors)
         slots = pl.ds(first_slot * rows, count * rows)
@@ -201,31 +212,42 @@
             weights.append(weight)
         summed = functools.reduce(jnp.add, weights)
         summed = jnp.broadcast_to(jnp.sum(summed, axis=1, keepdims=True), summed.shape)
-        mixed = jnp.dot(
-            jnp.concatenate([w.astype(jnp.bfloat16) for w in weights], axis=1),
-            vbuf[slots, columns],
+        weights = jnp.concatenate([w.astype(jnp.bfloat16) for w in weights], axis=1)
+        if not first:
+            summed = summed + tot[head] * fade
+        tot[head] = summed
+        if values_later:
+            late[head] = weights
+            acc[head] = acc[head] * fade
+            return
+        mixed = jnp.dot(weights, vbuf[slots, columns], preferred_element_type=jnp.float32)
+        if not first:
+            mixed = mixed + acc[head] * fade
+        top[head] = high
+        acc[head] = mixed
+
+    def per_head(unroll, step_of):
+        def body(index, carry):
+            for u in range(unroll):
+                step_of(index * unroll + u)
+            return carry
+
+        lax.fori_loop(0, HEADS // unroll, body, 0)
+
+    def group(first_slot, factors, first, values_later, unroll):
+        per_head(unroll, lambda head: head_group(head, first_slot, factors, first, values_later))
+
+    def late_values(head, which, last):
+        columns = pl.ds(pl.multiple_of(head * HEAD_DIM, HEAD_DIM), HEAD_DIM)
+        mixed = acc[head] + jnp.dot(
+            late[head, :, which * rows : (which + 1) * rows],
+            vbuf[pl.ds((DG + which) * rows, rows), columns],
             preferred_element_type=jnp.float32,
         )
-        if not first:
-            summed = summed + tot[head] * fade
-            mixed = mixed + acc[head] * fade
         if last:
-            out[:, columns] = (mixed / summed).astype(out.dtype)
+            mixed_heads[:, columns] = (mixed / tot[head]).astype(mixed_heads.dtype)
         else:
-            top[head] = high
-            tot[head] = summed
             acc[head] = mixed
-
-    def group(first_slot, factors, first, last, unroll):
-        def body(index, carry):
-            for u in range(unroll):
-                head_group(index * unroll + u, first_slot, factors, first, last)
-            return carry
-
-        if unroll == HEADS:
-            body(0, 0)
-        else:
-            lax.fori_loop(0, HEADS // unroll, body, 0)
 
     for load in loads:
         load.wait()
@@ -242,7 +264,8 @@
 
         @pl.when(gives_y)
         def _():
-            hand_y(kv).start()
+            hand_y(kv, 0).start()
+            hand_y(kv, 1).start()
 
         @pl.when(has_p)
         def _():
@@ -256,24 +279,41 @@
 
     group(YN, (0, 1, 2), False, False, 4)
 
-    for kv in range(2):
-
+    def diagonal(kv):
         @pl.when(has_m)
         def _():
             relay_y(kv).wait_recv()
+
+        @pl.when(has_m & gives_d)
+        def _():
+            hand_d(kv, 0).start()
+
+        @pl.when(has_m)
+        def _():
             relay_z(kv).wait_recv()
 
         @pl.when(has_m & gives_d)
         def _():
-            hand_d(kv).start()
-
-    for kv in range(2):
-
+            hand_d(kv, 1).start()
+
+    def handed(kv):
         @pl.when(x_valid)
         def _():
-            hand_y(kv).wait_recv()
-
+            hand_y(kv, 0).wait_recv()
+            hand_y(kv, 1).wait_recv()
+
+    diagonal(0)
+    handed(0)
     group(DG, (3, 4), False, True, 4)
+    load_w.wait()
+    diagonal(1)
+    per_head(HEADS, lambda head: late_values(head, 0, False))
+    handed(1)
+    per_head(HEADS, lambda head: late_values(head, 1, True))
+    for n in range(0, wv.shape[1], 512):
+        out[:, n : n + 512] = jnp.dot(
+            mixed_heads[...], wv[:, n : n + 512], preferred_element_type=jnp.float32
+        ).astype(out.dtype)
 
     for kv in range(2):
         to_sib(kv).wait_send()
@@ -291,18 +331,23 @@
 
         @pl.when(gives_y | has_m)
         def _():
-            hand_y(kv).wait_send()
-
-
-def attention(devices, queries, keys, values, far_picks):
+            hand_y(kv, 0).wait_send()
+            hand_y(kv, 1).wait_send()
+
+
+def attention(devices, queries, keys, values, far_picks, out_weight):
     rows, width = queries.shape
-    anywhere = pl.BlockSpec(memory_space=pl.ANY)
+    in_hbm = pl.BlockSpec(memory_space=pltpu.HBM)
     return pl.pallas_call(
         functools.partial(kernel, devices),
         out_shape=jax.ShapeDtypeStruct((rows, width), jnp.bfloat16),
-        in_specs=[pl.BlockSpec(memory_space=pltpu.SMEM), anywhere, anywhere, anywhere],
+        in_specs=[in_hbm] * 5,
         out_specs=pl.BlockSpec(memory_space=pltpu.VMEM),
         scratch_shapes=[
+            pltpu.SMEM(far_picks.shape, jnp.int32),
+            pltpu.VMEM((rows, width), jnp.bfloat16),
+            pltpu.VMEM(out_weight.shape, jnp.bfloat16),
+            pltpu.VMEM((HEADS, rows, 2 * rows), jnp.bfloat16),
             pltpu.VMEM((rows, width), jnp.bfloat16),
             pltpu.VMEM((7 * rows, width), jnp.bfloat16),
             pltpu.VMEM((7 * rows, width), jnp.bfloat16),
@@ -310,23 +355,22 @@
             pltpu.VMEM((HEADS, rows, HEAD_DIM), jnp.float32),
             pltpu.VMEM((HEADS, rows, HEAD_DIM), jnp.float32),
             pltpu.VMEM((HEADS, rows, HEAD_DIM), jnp.float32),
-            pltpu.SemaphoreType.DMA((3,)),
-            pltpu.SemaphoreType.DMA((7, 2)),
-            pltpu.SemaphoreType.DMA((7, 2)),
+            pltpu.SemaphoreType.DMA((5,)),
+            pltpu.SemaphoreType.DMA((8, 2)),
+            pltpu.SemaphoreType.DMA((8, 2)),
         ],
         compiler_params=pltpu.CompilerParams(
-            collective_id=0, has_side_effects=True, vmem_limit_bytes=24 * 1024 * 1024
+            collective_id=0, has_side_effects=True, vmem_limit_bytes=67_000_000
         ),
         name="relay_attention",
-    )(far_picks, queries, keys, values)
+    )(far_picks, queries, keys, values, out_weight)
 
 
 def solution(mesh):
     devices = mesh.shape["tm"]
 
     def body(queries, keys, values, far_picks, out_weight):
-        attended = attention(devices, queries, keys, values, far_picks)
-        return jnp.dot(attended, out_weight, preferred_element_type=jnp.float32).astype(jnp.bfloat16)
+        return attention(devices, queries, keys, values, far_picks, out_weight)
 
     placed = (
         P(("vid", "tm"), None),

time: 42.2 us -> 34.9 us (0.83)
  matrix products: 3.89 us -> 0 us
  local copies, waits for them, and re-layouts: 3.66 us -> 1.77 us
  Pallas kernels: 34.3 us -> 33 us
    dot_general x1 -> x0, matrix products: 3.89 us -> none  [body(): jnp.dot(attended, out_weight, preferred_element_type=jnp.float32)]
    unnamed x8 -> x1, local copies, waits for them, and re-layouts: 3.66 us -> 1.77 us
    pallas_call x1, Pallas kernels: 34.3 us -> 33 us  [attention(): pl.pallas_call(functools.partial(kernel, devices), out_shape=jax.ShapeDty...]
where the time goes in v2:
time: 34.9 us; the launch traced here: 34.8 us
  Pallas kernels  33 us (95%)
  local copies, waits for them, and re-layouts  1.77 us (5%)
    pallas_call x1, Pallas kernels, attention(): pl.pallas_call(functools.partial(kernel, devices), out_shape=jax.ShapeDty...  33 us
    unnamed x1, local copies, waits for them, and re-layouts  1.77 us

profile of v2, /device:TPU:15, one launch (start us, length us, event | category | flops | bytes accessed | tf_op | source)
XLA Modules:
  0.0 34.8 jit_solution(3885078259434716935)
XLA Ops:
  0.0 33.0 %relay_attention.1 = bf16[128,1536]{1,0:T(8,128)(2,1)} custom-call(s32[2,8]{1,0:T(2,128)} %picks_hbm.1, bf16[128,1536]{1,0:T(8,128)(2,1)} %q_hbm.1, bf16[128,1536]{1,0:T(8,128)(2,1)} %k_hbm.1, bf16[128,1536]{1,0:T(8,128)(2,1)} %v_hbm.1, bf16[1536,1536]{1,0:T(8,128)(2,1)} %w_hbm.1), custom_call_target="tpu_custom_call" | custom-call | tf_op jit(solution)/shard_map/relay_attention/pallas_call | solution.py:341
  33.0 1.8 %copy.7 = bf16[128,1536]{1,0:T(8,128)(2,1)} copy(bf16[128,1536]{1,0:T(8,128)(2,1)} %relay_attention.1) | data formatting | bytes 786432

commit v3 on v2

--- a/solution.py
+++ b/solution.py
@@ -15,6 +15,9 @@
 EXP_SCALE = HEAD_DIM ** (-0.5) * math.log2(math.e)
 OWN, SIB, YN, ZP, ZM, DG, XF = range(7)
 MESH = pl.DeviceIdType.MESH
+PIECES = ({0: (0, 6), 2: (6, 12)}, {0: (0, 4), 1: (4, 6), 2: (6, 10), 3: (10, 12)})
+BY_Y = ((0,), (0, 1))
+BY_Z = ((2,), (2, 3))
 
 
 def kernel(
@@ -30,6 +33,7 @@
     wv,
     late,
     mixed_heads,
+    projected,
     kbuf,
     vbuf,
     mult,
@@ -41,7 +45,6 @@
     recv_sem,
 ):
     rows = q_hbm.shape[0]
-    half = rows // 2
     chips = devices // 2
     p = lax.axis_index("tm")
     chip = p // 2
@@ -61,8 +64,10 @@
     def slot(buf, index):
         return buf.at[pl.ds(index * rows, rows)]
 
-    def part(buf, index, which):
-        return buf.at[pl.ds(index * rows + which * half, half)]
+    def part(kv, index, piece):
+        first, end = PIECES[kv][piece]
+        columns = pl.ds(first * HEAD_DIM, (end - first) * HEAD_DIM)
+        return bufs[kv].at[pl.ds(index * rows, rows), columns]
 
     def remote(src, dst, number, kv, dev):
         return pltpu.make_async_remote_copy(
@@ -89,17 +94,17 @@
     def to_zm(kv):
         return remote(hbms[kv], slot(bufs[kv], ZP), 3, kv, zm_dev)
 
-    def relay_y(kv):
-        return remote(part(bufs[kv], YN, 0), part(bufs[kv], DG, 0), 4, kv, zp_dev)
-
-    def relay_z(kv):
-        return remote(part(bufs[kv], ZP, 1), part(bufs[kv], DG, 1), 5, kv, y_dev)
-
-    def hand_y(kv, which):
-        return remote(part(bufs[kv], YN, which), part(bufs[kv], XF, which), 6 + which, kv, sib)
-
-    def hand_d(kv, which):
-        return remote(part(bufs[kv], DG, which), part(bufs[kv], XF, which), 6 + which, kv, sib)
+    def relay_y(kv, piece):
+        return remote(part(kv, YN, piece), part(kv, DG, piece), 4 + piece, kv, zp_dev)
+
+    def relay_z(kv, piece):
+        return remote(part(kv, ZP, piece), part(kv, DG, piece), 4 + piece, kv, y_dev)
+
+    def hand_y(kv, piece):
+        return remote(part(kv, YN, piece), part(kv, XF, piece), 8 + piece, kv, sib)
+
+    def hand_d(kv, piece):
+        return remote(part(kv, DG, piece), part(kv, XF, piece), 8 + piece, kv, sib)
 
     load_w = pltpu.make_async_copy(w_hbm, wv, load_sem.at[4])
     load_picks = pltpu.make_async_copy(picks_hbm, picks, load_sem.at[3])
@@ -238,7 +243,7 @@
         per_head(unroll, lambda head: head_group(head, first_slot, factors, first, values_later))
 
     def late_values(head, which, last):
-        columns = pl.ds(pl.multiple_of(head * HEAD_DIM, HEAD_DIM), HEAD_DIM)
+        columns = slice(head * HEAD_DIM, (head + 1) * HEAD_DIM)
         mixed = acc[head] + jnp.dot(
             late[head, :, which * rows : (which + 1) * rows],
             vbuf[pl.ds((DG + which) * rows, rows), columns],
@@ -260,17 +265,19 @@
 
         @pl.when(has_p)
         def _():
-            relay_y(kv).start()
+            for piece in BY_Y[kv]:
+                relay_y(kv, piece).start()
 
         @pl.when(gives_y)
         def _():
-            hand_y(kv, 0).start()
-            hand_y(kv, 1).start()
+            for piece in PIECES[kv]:
+                hand_y(kv, piece).start()
 
         @pl.when(has_p)
         def _():
             to_zm(kv).wait_recv()
-            relay_z(kv).start()
+            for piece in BY_Z[kv]:
+                relay_z(kv, piece).start()
 
     @pl.when(has_m)
     def _():
@@ -279,41 +286,53 @@
 
     group(YN, (0, 1, 2), False, False, 4)
 
-    def diagonal(kv):
+    def diagonal(kv, piece):
         @pl.when(has_m)
         def _():
-            relay_y(kv).wait_recv()
+            relay_y(kv, piece).wait_recv()
 
         @pl.when(has_m & gives_d)
         def _():
-            hand_d(kv, 0).start()
-
-        @pl.when(has_m)
-        def _():
-            relay_z(kv).wait_recv()
-
-        @pl.when(has_m & gives_d)
-        def _():
-            hand_d(kv, 1).start()
-
-    def handed(kv):
+            hand_d(kv, piece).start()
+
+    def handed(kv, piece):
         @pl.when(x_valid)
         def _():
-            hand_y(kv, 0).wait_recv()
-            hand_y(kv, 1).wait_recv()
-
-    diagonal(0)
-    handed(0)
+            hand_y(kv, piece).wait_recv()
+
+    def heads_of(pieces):
+        return [head for piece in pieces for head in range(*PIECES[1][piece])]
+
+    def project(pieces):
+        total = None
+        for piece in pieces:
+            first, end = PIECES[1][piece]
+            columns = slice(first * HEAD_DIM, end * HEAD_DIM)
+            term = jnp.dot(mixed_heads[:, columns], wv[columns, :], preferred_element_type=jnp.float32)
+            total = term if total is None else total + term
+        return total
+
+    for piece in PIECES[0]:
+        diagonal(0, piece)
+    for piece in PIECES[0]:
+        handed(0, piece)
     group(DG, (3, 4), False, True, 4)
     load_w.wait()
-    diagonal(1)
-    per_head(HEADS, lambda head: late_values(head, 0, False))
-    handed(1)
-    per_head(HEADS, lambda head: late_values(head, 1, True))
-    for n in range(0, wv.shape[1], 512):
-        out[:, n : n + 512] = jnp.dot(
-            mixed_heads[...], wv[:, n : n + 512], preferred_element_type=jnp.float32
-        ).astype(out.dtype)
+    early, final = (0, 2), (1, 3)
+    for pieces in (early, final):
+        for piece in pieces:
+            diagonal(1, piece)
+        for head in heads_of(pieces):
+            late_values(head, 0, False)
+    for pieces in (early, final):
+        for piece in pieces:
+            handed(1, piece)
+        for head in heads_of(pieces):
+            late_values(head, 1, True)
+        if pieces is early:
+            projected[...] = project(pieces)
+        else:
+            out[...] = (projected[...] + project(pieces)).astype(out.dtype)
 
     for kv in range(2):
         to_sib(kv).wait_send()
@@ -322,8 +341,10 @@
         @pl.when(has_p)
         def _():
             to_zp(kv).wait_send()
-            relay_y(kv).wait_send()
-            relay_z(kv).wait_send()
+            for piece in BY_Y[kv]:
+                relay_y(kv, piece).wait_send()
+            for piece in BY_Z[kv]:
+                relay_z(kv, piece).wait_send()
 
         @pl.when(has_m)
         def _():
@@ -331,8 +352,8 @@
 
         @pl.when(gives_y | has_m)
         def _():
-            hand_y(kv, 0).wait_send()
-            hand_y(kv, 1).wait_send()
+            for piece in PIECES[kv]:
+                hand_y(kv, piece).wait_send()
 
 
 def attention(devices, queries, keys, values, far_picks, out_weight):
@@ -349,6 +370,7 @@
             pltpu.VMEM(out_weight.shape, jnp.bfloat16),
             pltpu.VMEM((HEADS, rows, 2 * rows), jnp.bfloat16),
             pltpu.VMEM((rows, width), jnp.bfloat16),
+            pltpu.VMEM((rows, width), jnp.float32),
             pltpu.VMEM((7 * rows, width), jnp.bfloat16),
             pltpu.VMEM((7 * rows, width), jnp.bfloat16),
             pltpu.VMEM((5, rows, rows), jnp.float32),
@@ -356,8 +378,8 @@
             pltpu.VMEM((HEADS, rows, HEAD_DIM), jnp.float32),
             pltpu.VMEM((HEADS, rows, HEAD_DIM), jnp.float32),
             pltpu.SemaphoreType.DMA((5,)),
-            pltpu.SemaphoreType.DMA((8, 2)),
-            pltpu.SemaphoreType.DMA((8, 2)),
+            pltpu.SemaphoreType.DMA((12, 2)),
+            pltpu.SemaphoreType.DMA((12, 2)),
         ],
         compiler_params=pltpu.CompilerParams(
             collective_id=0, has_side_effects=True, vmem_limit_bytes=67_000_000

time: 34.9 us -> 34.4 us (0.986)
  Pallas kernels: 33 us -> 32.5 us
    pallas_call x1, Pallas kernels: 33 us -> 32.5 us  [attention(): pl.pallas_call(functools.partial(kernel, devices), out_shape=jax.ShapeDty...]
where the time goes in v3:
time: 34.4 us; the launch traced here: 34.3 us
  Pallas kernels  32.5 us (94%)
  local copies, waits for them, and re-layouts  1.77 us (5%)
    pallas_call x1, Pallas kernels, attention(): pl.pallas_call(functools.partial(kernel, devices), out_shape=jax.ShapeDty...  32.5 us
    unnamed x1, local copies, waits for them, and re-layouts  1.77 us

profile of v3, /device:TPU:15, one launch (start us, length us, event | category | flops | bytes accessed | tf_op | source)
XLA Modules:
  0.0 34.3 jit_solution(4639974293384877268)
XLA Ops:
  0.0 32.5 %relay_attention.1 = bf16[128,1536]{1,0:T(8,128)(2,1)} custom-call(s32[2,8]{1,0:T(2,128)} %picks_hbm.1, bf16[128,1536]{1,0:T(8,128)(2,1)} %q_hbm.1, bf16[128,1536]{1,0:T(8,128)(2,1)} %k_hbm.1, bf16[128,1536]{1,0:T(8,128)(2,1)} %v_hbm.1, bf16[1536,1536]{1,0:T(8,128)(2,1)} %w_hbm.1), custom_call_target="tpu_custom_call" | custom-call | tf_op jit(solution)/shard_map/relay_attention/pallas_call | solution.py:362
  32.5 1.8 %copy.7 = bf16[128,1536]{1,0:T(8,128)(2,1)} copy(bf16[128,1536]{1,0:T(8,128)(2,1)} %relay_attention.1) | data formatting | bytes 786432

commit v4 on v3

--- a/solution.py
+++ b/solution.py
@@ -231,16 +231,21 @@
         top[head] = high
         acc[head] = mixed
 
-    def per_head(unroll, step_of):
+    def per_head(unroll, step_of, first=0, end=HEADS):
         def body(index, carry):
             for u in range(unroll):
                 step_of(index * unroll + u)
             return carry
 
-        lax.fori_loop(0, HEADS // unroll, body, 0)
-
-    def group(first_slot, factors, first, values_later, unroll):
-        per_head(unroll, lambda head: head_group(head, first_slot, factors, first, values_later))
+        lax.fori_loop(first // unroll, end // unroll, body, 0)
+
+    def group(first_slot, factors, first, values_later, unroll, start=0, end=HEADS):
+        per_head(
+            unroll,
+            lambda head: head_group(head, first_slot, factors, first, values_later),
+            start,
+            end,
+        )
 
     def late_values(head, which, last):
         columns = slice(head * HEAD_DIM, (head + 1) * HEAD_DIM)
@@ -263,7 +268,7 @@
     for kv in range(2):
         to_y(kv).wait_recv()
 
-        @pl.when(has_p)
+        @pl.when(has_p & (gives_d | (kv == 0)))
         def _():
             for piece in BY_Y[kv]:
                 relay_y(kv, piece).start()
@@ -276,6 +281,9 @@
         @pl.when(has_p)
         def _():
             to_zm(kv).wait_recv()
+
+        @pl.when(has_p & (gives_y | (kv == 0)))
+        def _():
             for piece in BY_Z[kv]:
                 relay_z(kv, piece).start()
 
@@ -284,7 +292,19 @@
         for kv in range(2):
             to_zp(kv).wait_recv()
 
-    group(YN, (0, 1, 2), False, False, 4)
+    group(YN, (0, 1, 2), False, False, 4, 0, 4)
+
+    @pl.when(has_p & gives_y)
+    def _():
+        for piece in BY_Y[1]:
+            relay_y(1, piece).start()
+
+    @pl.when(has_p & gives_d)
+    def _():
+        for piece in BY_Z[1]:
+            relay_z(1, piece).start()
+
+    group(YN, (0, 1, 2), False, False, 4, 4, HEADS)
 
     def diagonal(kv, piece):
         @pl.when(has_m)

time: 34.4 us -> 34.4 us (level)
  no operation moved by 1% of the time
where the time goes in v4:
time: 34.4 us; the launch traced here: 34.3 us
  Pallas kernels  32.5 us (94%)
  local copies, waits for them, and re-layouts  1.77 us (5%)
    pallas_call x1, Pallas kernels, attention(): pl.pallas_call(functools.partial(kernel, devices), out_shape=jax.ShapeDty...  32.5 us
    unnamed x1, local copies, waits for them, and re-layouts  1.77 us

profile of v4, /device:TPU:15, one launch (start us, length us, event | category | flops | bytes accessed | tf_op | source)
XLA Modules:
  0.0 34.3 jit_solution(14304682699565671804)
XLA Ops:
  0.0 32.5 %relay_attention.1 = bf16[128,1536]{1,0:T(8,128)(2,1)} custom-call(s32[2,8]{1,0:T(2,128)} %picks_hbm.1, bf16[128,1536]{1,0:T(8,128)(2,1)} %q_hbm.1, bf16[128,1536]{1,0:T(8,128)(2,1)} %k_hbm.1, bf16[128,1536]{1,0:T(8,128)(2,1)} %v_hbm.1, bf16[1536,1536]{1,0:T(8,128)(2,1)} %w_hbm.1), custom_call_target="tpu_custom_call" | custom-call | tf_op jit(solution)/shard_map/relay_attention/pallas_call | solution.py:382
  32.5 1.8 %copy.7 = bf16[128,1536]{1,0:T(8,128)(2,1)} copy(bf16[128,1536]{1,0:T(8,128)(2,1)} %relay_attention.1) | data formatting | bytes 786432
